TPU v7x, 32 devices: a whole 2x2x4 slice. The times are simulated.
32 devices in a mesh: group: 2 (over y), patch: 4 (over z), head: 2 (over x), cfg: 2 (over core).
Axes of the slice: x: 2, y: 2, z: 4, core: 2. Of those that a mesh axis runs over, the one named last changes fastest.
Arguments:
- fresh_query: bfloat16 [4, 256, 2560], P(('group', 'cfg'), ('patch', 'head')), parts along dimension 0, may hold values from -32 to 32
- fresh_key: bfloat16 [4, 256, 2560], P(('group', 'cfg'), ('patch', 'head')), parts along dimension 0, may hold values from -9 to 9
- fresh_value: bfloat16 [4, 256, 2560], P(('group', 'cfg'), ('patch', 'head')), parts along dimension 0, may hold values from -12 to 12
- stale_key: bfloat16 [4, 256, 2560], P(('group', 'cfg'), 'patch', 'head'), parts along dimension 0, may hold values from -8 to 8
- stale_value: bfloat16 [4, 256, 2560], P(('group', 'cfg'), 'patch', 'head'), parts along dimension 0, may hold values from -12 to 12
- cross_query: bfloat16 [4, 256, 2560], P(('group', 'cfg'), ('patch', 'head')), parts along dimension 0, may hold values from -32 to 32
- text_key: bfloat16 [4, 512, 2560], P(('group', 'cfg'), None, 'head'), parts along dimension 0, may hold values from -8 to 8
- text_value: bfloat16 [4, 512, 2560], P(('group', 'cfg'), None, 'head'), parts along dimension 0, may hold values from -12 to 12
- text_mask: int32 [4, 512], P(('group', 'cfg')), parts along dimension 0, may hold values from 0 to 1, as said below
Outputs:
- self_mixed: bfloat16 [4, 256, 2560], P(('group', 'cfg'), ('patch', 'head')), parts along dimension 0
- cross_mixed: bfloat16 [4, 256, 2560], P(('group', 'cfg'), ('patch', 'head')), parts along dimension 0
There are 2 independent parts, one for each index of `group`. A program takes and returns all parts, laid end to end along the dimension named above; each array names one. Nothing has to cross between parts.
Inputs may be any that keep to these rules, and one draw needn't show every extreme that they name: In each branch the ones of text_mask form a prefix of 32 or more positions; in one of the two branches all 512 are ones, in the other some are zeros.
All inputs are finite; a program needn't handle non-finite values.
Results may differ from a plain program's by a relative error of at most 0.005.
Values may be sent and summed in bfloat16 or wider, within the bound.
A program may use at most 128 MiB of HBM per device.

v0:
```python
import functools
import math

import jax
import jax.numpy as jnp
from jax import lax
from jax.experimental import pallas as pl
from jax.experimental.pallas import tpu as pltpu
from jax.sharding import PartitionSpec as P

HD = 128
MESH = pl.DeviceIdType.MESH


def dot_nt(a, b):
    return lax.dot_general(a, b, (((1,), (1,)), ((), ())), preferred_element_type=jnp.float32)


def kernel(
    n_patch, n_head, nch,
    fq, fk, fv, sk, sv, cq, tk, tv, mask,
    so, co,
    fx, kv, txk, txv, mk, outs, outc,
    x_send, x_recv, x_loc, t_loc, kv_loc, own_send, fwd_send, kv_recv,
    o_send, o_recv, o_loc, c_send, c_recv, c_loc,
    dq, part_out, part_in, stat_out, stat_in, dq_sem, part_send, part_recv,
):
    p = lax.axis_index("patch")
    h = lax.axis_index("head")
    rows = fq.shape[1]
    prows = rows * n_head
    hcols = sk.shape[2]
    ccols = hcols // nch
    heads = hcols // HD
    cheads = heads // nch
    scale = 1.0 / math.sqrt(HD)
    fresh = (cq, fq, fk, fv)
    my_rows = pl.ds(pl.multiple_of(h * rows, rows), rows)

    for c in range(nch):
        for i, ref in enumerate((sk, sv)):
            pltpu.make_async_copy(
                ref.at[0, :, pl.ds(c * ccols, ccols)], kv.at[p, c, i], kv_loc.at[c, i]
            ).start()
    text_copies = [
        pltpu.make_async_copy(mask, mk, t_loc.at[0]),
        pltpu.make_async_copy(tk.at[0], txk, t_loc.at[1]),
        pltpu.make_async_copy(tv.at[0], txv, t_loc.at[2]),
    ]
    own_copies = [
        pltpu.make_async_copy(
            ref.at[0, :, pl.ds(pl.multiple_of(h * hcols, hcols), hcols)],
            fx.at[a, my_rows, :],
            x_loc.at[a],
        )
        for a, ref in enumerate(fresh)
    ]
    for cp in own_copies + text_copies:
        cp.start()

    barrier = pltpu.get_barrier_semaphore()
    has_right = p < n_patch - 1
    has_left = p > 0

    @pl.when(has_right)
    def _():
        pl.semaphore_signal(barrier, inc=1, device_id={"patch": p + 1}, device_id_type=MESH)

    @pl.when(has_left)
    def _():
        pl.semaphore_signal(barrier, inc=1, device_id={"patch": p - 1}, device_id_type=MESH)

    for k in range(1, n_head):
        pl.semaphore_signal(
            barrier, inc=1, device_id={"head": lax.rem(h + k, n_head)}, device_id_type=MESH
        )
    pl.semaphore_wait(
        barrier, n_head - 1 + has_right.astype(jnp.int32) + has_left.astype(jnp.int32)
    )

    def x_copy(a, k):
        peer = lax.rem(h + k, n_head)
        return pltpu.make_async_remote_copy(
            src_ref=fresh[a].at[0, :, pl.ds(pl.multiple_of(peer * hcols, hcols), hcols)],
            dst_ref=fx.at[a, my_rows, :],
            send_sem=x_send.at[a, k - 1],
            recv_sem=x_recv.at[a, k - 1],
            device_id={"head": peer},
            device_id_type=MESH,
        )

    def kv_copy(src, c, target, sem):
        return pltpu.make_async_remote_copy(
            src_ref=kv.at[src, c],
            dst_ref=kv.at[src, c],
            send_sem=sem,
            recv_sem=kv_recv.at[src, c],
            device_id={"patch": target},
            device_id_type=MESH,
        )

    def start_x():
        for a in (1, 0, 2, 3):
            for k in range(1, n_head):
                x_copy(a, k).start()

    def wait_own_kv(c):
        for i, ref in enumerate((sk, sv)):
            pltpu.make_async_copy(
                ref.at[0, :, pl.ds(c * ccols, ccols)], kv.at[p, c, i], kv_loc.at[c, i]
            ).wait()

    def wait_x(a):
        own_copies[a].wait()
        for k in range(1, n_head):
            x_copy(a, k).wait_recv()

    def out_copy(src, dst, c, k, send, recv):
        peer = lax.rem(h + k, n_head)
        return pltpu.make_async_remote_copy(
            src_ref=src.at[c, pl.ds(pl.multiple_of(peer * rows, rows), rows), :],
            dst_ref=dst.at[0, :, pl.ds(pl.multiple_of(h * hcols + c * ccols, HD), ccols)],
            send_sem=send.at[c, k - 1],
            recv_sem=recv.at[c, k - 1],
            device_id={"head": peer},
            device_id_type=MESH,
        )

    def local_out(src, dst, c, sem):
        return pltpu.make_async_copy(
            src.at[c, my_rows, :],
            dst.at[0, :, pl.ds(pl.multiple_of(h * hcols + c * ccols, HD), ccols)],
            sem.at[c],
        )

    def send_out(src, dst, c, send, recv, loc):
        for k in range(1, n_head):
            out_copy(src, dst, c, k, send, recv).start()
        local_out(src, dst, c, loc).start()

    def cross_chunk(c):
        usable = mk[...] > 0
        for i in range(cheads):
            cols = pl.ds((c * cheads + i) * HD, HD)
            scores = dot_nt(fx[0, :, cols], txk[:, cols]) * scale
            scores = jnp.where(usable, scores, -jnp.inf)
            top = jnp.max(scores, axis=-1, keepdims=True)
            weights = jnp.exp(scores - top)
            total = jnp.sum(weights, axis=-1, keepdims=True)
            mix = jnp.dot(
                weights.astype(jnp.bfloat16), txv[:, cols], preferred_element_type=jnp.float32
            )
            outc[c, :, i * HD : (i + 1) * HD] = (mix / total).astype(jnp.bfloat16)

    def query(j):
        return fx[1, :, pl.ds(j * HD, HD)]

    def weigh(q, keys, values, top=None):
        scores = dot_nt(q, keys) * scale
        new_top = jnp.max(scores, axis=-1, keepdims=True)
        if top is not None:
            new_top = jnp.maximum(top, new_top)
        weights = jnp.exp(scores - new_top).astype(jnp.bfloat16)
        wide = jnp.concatenate([values, jnp.ones_like(values)], axis=1)
        mixed = jnp.dot(weights, wide, preferred_element_type=jnp.float32)
        return new_top, mixed[:, HD:], mixed[:, :HD]

    def absorb_rows(state, q, keys, values):
        top, total, mix = state
        new_top, more_total, more_mix = weigh(q, keys, values, top)
        factor = jnp.exp(top - new_top)
        return new_top, total * factor + more_total, mix * factor + more_mix

    def kv_rows(i, j, *sources):
        c, k = divmod(j, cheads)
        parts = [kv[src, c, i, :, pl.ds(k * HD, HD)] for src in sources]
        return parts[0] if len(parts) == 1 else jnp.concatenate(parts, axis=0)

    def fresh_rows(i, j):
        return fx[2 + i, :, pl.ds(j * HD, HD)]

    def first(j):
        return weigh(query(j), fresh_rows(0, j), fresh_rows(1, j))

    def absorb(state, src, j):
        return absorb_rows(state, query(j), kv_rows(0, j, src), kv_rows(1, j, src))

    def line_program():
        start_x()
        for c in range(nch):
            wait_own_kv(c)

            @pl.when(has_right)
            def _():
                kv_copy(p, c, p + 1, own_send.at[0, c]).start()

            @pl.when(has_left)
            def _():
                kv_copy(p, c, p - 1, own_send.at[1, c]).start()

        shorter = jnp.minimum(p, n_patch - 1 - p)

        def slot_source(s):
            near = s // 2 + 1
            near_src = jnp.where(s % 2 == 0, p - near, p + near)
            far = s - shorter + 1
            far_src = jnp.where(p > shorter, p - far, p + far)
            return jnp.where(s < 2 * shorter, near_src, far_src)

        def forward_target(src):
            target = jnp.where(src < p, p + 1, p - 1)
            return target, (target >= 0) & (target < n_patch)

        def forward(s, c):
            src = slot_source(s)
            kv_copy(src, c, p, fwd_send.at[s, c]).wait_recv()
            target, valid = forward_target(src)

            @pl.when(valid)
            def _():
                kv_copy(src, c, target, fwd_send.at[s, c]).start()

        half = (nch + 1) // 2
        for cp in text_copies:
            cp.wait()
        wait_x(0)
        for c in range(half):
            cross_chunk(c)
        for c in range(half):
            forward(0, c)
        for c in range(half, nch):
            cross_chunk(c)
        for c in range(nch):
            send_out(outc, co, c, c_send, c_recv, c_loc)
        for c in range(half, nch):
            forward(0, c)
        for a in range(1, 4):
            wait_x(a)
        states = [first(j) for j in range(heads)]
        src = slot_source(0)
        states = [absorb(states[j], src, j) for j in range(heads)]

        def slot(s, states):
            src = slot_source(s)
            out = []
            for c in range(nch):
                forward(s, c)
                for j in range(c * cheads, (c + 1) * cheads):
                    out.append(absorb(states[j], src, j))
            return out

        if n_patch <= 8:
            for s in range(1, n_patch - 2):
                states = slot(s, states)
        else:
            states = lax.fori_loop(1, n_patch - 2, slot, states)
        last = n_patch - 2
        src = slot_source(last)
        for c in range(nch):
            if last > 0:
                forward(last, c)
            for i in range(cheads):
                j = c * cheads + i
                _, total, mix = absorb(states[j], src, j) if last > 0 else states[j]
                outs[c, :, i * HD : (i + 1) * HD] = (mix / total).astype(jnp.bfloat16)
            if c > 0:
                send_out(outs, so, c - 1, o_send, o_recv, o_loc)
        send_out(outs, so, nch - 1, o_send, o_recv, o_loc)

        for c in range(nch):

            @pl.when(has_right)
            def _():
                kv_copy(p, c, p + 1, own_send.at[0, c]).wait_send()

            @pl.when(has_left)
            def _():
                kv_copy(p, c, p - 1, own_send.at[1, c]).wait_send()

        def drain(s, carry):
            for c in range(nch):
                target, valid = forward_target(slot_source(s))

                @pl.when(valid)
                def _():
                    kv_copy(slot_source(s), c, target, fwd_send.at[s, c]).wait_send()

            return carry

        if n_patch <= 8:
            for s in range(n_patch - 1):
                drain(s, 0)
        else:
            lax.fori_loop(0, n_patch - 1, drain, 0)

    is_end = jnp.logical_not(has_right & has_left)
    across = n_patch - 1 - p
    lanes = lax.broadcasted_iota(jnp.int32, (prows, HD), 1)

    early = (cheads + 1) // 2

    def neighbour(c, other):
        return [
            pltpu.make_async_remote_copy(
                src_ref=src.at[c, :, pl.ds(at, size)],
                dst_ref=dst.at[c, :, pl.ds(at, size)],
                send_sem=part_send.at[c, i],
                recv_sem=part_recv.at[c, i],
                device_id={"patch": other},
                device_id_type=MESH,
            )
            for i, (src, dst, at, size) in enumerate(
                (
                    (part_out, part_in, 0, early * HD),
                    (part_out, part_in, early * HD, (cheads - early) * HD),
                    (stat_out, stat_in, 0, HD),
                )
            )
        ]

    def dq_copy(other):
        return pltpu.make_async_remote_copy(
            src_ref=fx.at[1],
            dst_ref=dq,
            send_sem=dq_sem.at[0],
            recv_sem=dq_sem.at[1],
            device_id={"patch": other},
            device_id_type=MESH,
        )

    def end_program():
        helper = jnp.where(has_right, p + 1, p - 1)
        lead = min(2, nch)
        for c in range(lead):
            wait_own_kv(c)
            kv_copy(p, c, helper, own_send.at[0, c]).start()
        start_x()
        wait_x(1)
        dq_copy(helper).start()
        for c in range(lead, nch):
            wait_own_kv(c)
            kv_copy(p, c, helper, own_send.at[0, c]).start()
        for cp in text_copies:
            cp.wait()
        wait_x(0)
        for c in range(nch):
            cross_chunk(c)
            if c > 0:
                send_out(outc, co, c - 1, c_send, c_recv, c_loc)
        send_out(outc, co, nch - 1, c_send, c_recv, c_loc)
        wait_x(2)
        wait_x(3)
        states = [first(j) for j in range(heads)]
        for c in range(nch):
            for cp in neighbour(c, helper):
                cp.wait_recv()
            for i in range(cheads):
                top, total, mix = states[c * cheads + i]
                cols = slice(i * HD, (i + 1) * HD)
                lse = stat_in[c, :, i : i + 1]
                new_top = jnp.maximum(top, lse)
                mine = jnp.exp(top - new_top)
                theirs = jnp.exp(lse - new_top)
                mix = mix * mine + part_in[c, :, cols].astype(jnp.float32) * theirs
                outs[c, :, cols] = (mix / (total * mine + theirs)).astype(jnp.bfloat16)
            send_out(outs, so, c, o_send, o_recv, o_loc)
        for c in range(nch):
            kv_copy(p, c, helper, own_send.at[0, c]).wait_send()
        dq_copy(helper).wait_send()

    def helper_program():
        end = jnp.where(p < across, p - 1, p + 1)
        far = n_patch - 1 - end
        for c in range(nch):
            wait_own_kv(c)
            kv_copy(p, c, across, own_send.at[0, c]).start()

        start_x()

        def pass_on(c):
            kv_copy(end, c, across, fwd_send.at[0, c]).wait_recv()
            kv_copy(end, c, across, fwd_send.at[0, c]).start()

        pass_on(0)
        for cp in text_copies:
            cp.wait()
        wait_x(0)
        for c in range(nch):
            cross_chunk(c)
            if c > 0:
                send_out(outc, co, c - 1, c_send, c_recv, c_loc)
            if c + 1 < nch:
                pass_on(c + 1)
        send_out(outc, co, nch - 1, c_send, c_recv, c_loc)
        for a in range(1, 4):
            wait_x(a)
        dq_copy(end).wait_recv()

        def both(j):
            return jnp.concatenate([query(j), dq[:, pl.ds(j * HD, HD)]], axis=0)

        states = []
        for j in range(heads):
            mine = weigh(
                query(j),
                jnp.concatenate([fresh_rows(0, j), kv_rows(0, j, end)], axis=0),
                jnp.concatenate([fresh_rows(1, j), kv_rows(1, j, end)], axis=0),
            )
            theirs = weigh(dq[:, pl.ds(j * HD, HD)], kv_rows(0, j, p), kv_rows(1, j, p))
            states.append([jnp.concatenate(pair, axis=0) for pair in zip(mine, theirs)])
        for c in range(nch):
            kv_copy(across, c, p, own_send.at[0, c]).wait_recv()
        for c in range(nch):
            kv_copy(far, c, p, own_send.at[0, c]).wait_recv()
            stat = jnp.zeros((prows, HD), jnp.float32)
            for i in range(cheads):
                j = c * cheads + i
                top, total, mix = absorb_rows(
                    states[j], both(j), kv_rows(0, j, across, far), kv_rows(1, j, across, far)
                )
                mixed = (mix / total).astype(jnp.bfloat16)
                lse = top[prows:] + jnp.log(total[prows:])
                stat = jnp.where(lanes == i, lse, stat)
                part_out[c, :, i * HD : (i + 1) * HD] = mixed[prows:]
                outs[c, :, i * HD : (i + 1) * HD] = mixed[:prows]
                if i == early - 1:
                    neighbour(c, end)[0].start()
            stat_out[c] = stat
            for cp in neighbour(c, end)[1:]:
                cp.start()
            send_out(outs, so, c, o_send, o_recv, o_loc)
        for c in range(nch):
            kv_copy(p, c, across, own_send.at[0, c]).wait_send()
            kv_copy(end, c, across, fwd_send.at[0, c]).wait_send()
            for cp in neighbour(c, end):
                cp.wait_send()

    if n_patch == 4:
        pl.when(is_end)(end_program)
        pl.when(jnp.logical_not(is_end))(helper_program)
    else:
        line_program()

    for a in range(4):
        for k in range(1, n_head):
            x_copy(a, k).wait_send()
    for src_ref, dst, send, recv, loc in (
        (outc, co, c_send, c_recv, c_loc),
        (outs, so, o_send, o_recv, o_loc),
    ):
        for c in range(nch):
            for k in range(1, n_head):
                cp = out_copy(src_ref, dst, c, k, send, recv)
                cp.wait_send()
                cp.wait_recv()
            local_out(src_ref, dst, c, loc).wait()


def store_kernel(a, b, so, co, sem):
    copies = [
        pltpu.make_async_copy(a, so, sem.at[0]),
        pltpu.make_async_copy(b, co, sem.at[1]),
    ]
    for cp in copies:
        cp.start()
    for cp in copies:
        cp.wait()


def store(a, b):
    return pl.pallas_call(
        store_kernel,
        out_shape=(
            jax.ShapeDtypeStruct(a.shape, a.dtype),
            jax.ShapeDtypeStruct(b.shape, b.dtype),
        ),
        in_specs=[pl.BlockSpec(memory_space=pltpu.VMEM)] * 2,
        out_specs=(pl.BlockSpec(memory_space=pltpu.HBM),) * 2,
        scratch_shapes=[pltpu.SemaphoreType.DMA((2,))],
        compiler_params=pltpu.CompilerParams(vmem_limit_bytes=1024 * 1024),
        name="store_outputs",
    )(a, b)


def per_device(n_patch, n_head, *args):
    fq, fk, fv, sk, sv, cq, tk, tv, mask = args
    rows = fq.shape[1]
    prows = rows * n_head
    hcols = sk.shape[2]
    heads = hcols // HD
    nch = 2 if heads % 2 == 0 else 1
    ccols = hcols // nch
    txt = tk.shape[1]
    peers = max(n_head - 1, 1)
    any_spec = pl.BlockSpec(memory_space=pl.ANY)
    dma = pltpu.SemaphoreType.DMA
    bf16 = jnp.bfloat16
    mixed = pl.pallas_call(
        functools.partial(kernel, n_patch, n_head, nch),
        out_shape=(
            pltpu.VMEM(fq.shape, bf16),
            pltpu.VMEM(cq.shape, bf16),
        ),
        in_specs=[any_spec] * 9,
        out_specs=(pl.BlockSpec(memory_space=pltpu.VMEM),) * 2,
        scratch_shapes=[
            pltpu.VMEM((4, prows, hcols), bf16),
            pltpu.VMEM((n_patch, nch, 2, prows, ccols), bf16),
            pltpu.VMEM((txt, hcols), bf16),
            pltpu.VMEM((txt, hcols), bf16),
            pltpu.VMEM((1, txt), jnp.int32),
            pltpu.VMEM((nch, prows, ccols), bf16),
            pltpu.VMEM((nch, prows, ccols), bf16),
            dma((4, peers)),
            dma((4, peers)),
            dma((4,)),
            dma((3,)),
            dma((nch, 2)),
            dma((2, nch)),
            dma((n_patch, nch)),
            dma((n_patch, nch)),
            dma((nch, peers)),
            dma((nch, peers)),
            dma((nch,)),
            dma((nch, peers)),
            dma((nch, peers)),
            dma((nch,)),
            pltpu.VMEM((prows, hcols), bf16),
            pltpu.VMEM((nch, prows, ccols), bf16),
            pltpu.VMEM((nch, prows, ccols), bf16),
            pltpu.VMEM((nch, prows, HD), jnp.float32),
            pltpu.VMEM((nch, prows, HD), jnp.float32),
            dma((2,)),
            dma((nch, 3)),
            dma((nch, 3)),
        ],
        compiler_params=pltpu.CompilerParams(collective_id=0, has_side_effects=True),
        name="displaced_attention",
    )(*args)
    return store(*mixed)


def solution(mesh):
    return jax.shard_map(
        functools.partial(per_device, mesh.shape["patch"], mesh.shape["head"]),
        mesh=mesh,
        in_specs=(
            P(("group", "cfg"), ("patch", "head"), None),
            P(("group", "cfg"), ("patch", "head"), None),
            P(("group", "cfg"), ("patch", "head"), None),
            P(("group", "cfg"), "patch", "head"),
            P(("group", "cfg"), "patch", "head"),
            P(("group", "cfg"), ("patch", "head"), None),
            P(("group", "cfg"), None, "head"),
            P(("group", "cfg"), None, "head"),
            P(("group", "cfg"), None),
        ),
        out_specs=(
            P(("group", "cfg"), ("patch", "head"), None),
            P(("group", "cfg"), ("patch", "head"), None),
        ),
        check_vma=False,
    )
```

profile of v0, /device:TPU:0, one launch (start us, length us, event | category | flops | bytes accessed | tf_op | source)
XLA Modules:
  0.0 31.1 jit_solution(3708170898712100400)
XLA Ops:
  0.6 29.7 %displaced_attention.1 = (bf16[1,32,2560]{2,1,0:T(8,128)(2,1)S(1)}, bf16[1,32,2560]{2,1,0:T(8,128)(2,1)S(1)}) custom-call(bf16[1,32,2560]{2,1,0:T(8,128)(2,1)} %fq.1, bf16[1,32,2560]{2,1,0:T(8,128)(2,1)} %fk.1, bf16[1,32,2560]{2,1,0:T(8,128)(2,1)} %fv.1, bf16[1,64,1280]{2,1,0:T(8,128)(2,1)} %sk.1, bf16[1,64,1280]{2,1,0:T(8,128)(2,1)} %sv.1, ...), custom_call_target="tpu_custom_call" | custom-call | tf_op jit(solution)/shard_map/displaced_attention/pallas_call | solution.py:498
  30.3 0.7 %store_outputs.1 = (bf16[1,32,2560]{2,1,0:T(8,128)(2,1)}, bf16[1,32,2560]{2,1,0:T(8,128)(2,1)}) custom-call(bf16[1,32,2560]{2,1,0:T(8,128)(2,1)S(1)} %get-tuple-element.4.a, bf16[1,32,2560]{2,1,0:T(8,128)(2,1)S(1)} %get-tuple-element.5.b), custom_call_target="tpu_custom_call" | custom-call | tf_op jit(solution)/shard_map/store_outputs/pallas_call | solution.py:471
where the time goes:
time: 31.2 us; the launch traced here: 31.1 us
  Pallas kernels  30.4 us (97%)
  between operations  0.64 us (2%)
    pallas_call x1, Pallas kernels, per_device(): pl.pallas_call(functools.partial(kernel, n_patch, n_head, nch), out_shape...  29.7 us
    pallas_call x1, Pallas kernels, store(): pl.pallas_call(store_kernel, out_shape=(jax.ShapeDtypeStruct(a.shape, a.d...  0.74 us

commit v1 on v0

--- a/solution.py
+++ b/solution.py
@@ -16,14 +16,13 @@
     return lax.dot_general(a, b, (((1,), (1,)), ((), ())), preferred_element_type=jnp.float32)
 
 
-def kernel(
+def line_kernel(
     n_patch, n_head, nch,
     fq, fk, fv, sk, sv, cq, tk, tv, mask,
     so, co,
     fx, kv, txk, txv, mk, outs, outc,
     x_send, x_recv, x_loc, t_loc, kv_loc, own_send, fwd_send, kv_recv,
     o_send, o_recv, o_loc, c_send, c_recv, c_loc,
-    dq, part_out, part_in, stat_out, stat_in, dq_sem, part_send, part_recv,
 ):
     p = lax.axis_index("patch")
     h = lax.axis_index("head")
@@ -293,153 +292,7 @@
         else:
             lax.fori_loop(0, n_patch - 1, drain, 0)
 
-    is_end = jnp.logical_not(has_right & has_left)
-    across = n_patch - 1 - p
-    lanes = lax.broadcasted_iota(jnp.int32, (prows, HD), 1)
-
-    early = (cheads + 1) // 2
-
-    def neighbour(c, other):
-        return [
-            pltpu.make_async_remote_copy(
-                src_ref=src.at[c, :, pl.ds(at, size)],
-                dst_ref=dst.at[c, :, pl.ds(at, size)],
-                send_sem=part_send.at[c, i],
-                recv_sem=part_recv.at[c, i],
-                device_id={"patch": other},
-                device_id_type=MESH,
-            )
-            for i, (src, dst, at, size) in enumerate(
-                (
-                    (part_out, part_in, 0, early * HD),
-                    (part_out, part_in, early * HD, (cheads - early) * HD),
-                    (stat_out, stat_in, 0, HD),
-                )
-            )
-        ]
-
-    def dq_copy(other):
-        return pltpu.make_async_remote_copy(
-            src_ref=fx.at[1],
-            dst_ref=dq,
-            send_sem=dq_sem.at[0],
-            recv_sem=dq_sem.at[1],
-            device_id={"patch": other},
-            device_id_type=MESH,
-        )
-
-    def end_program():
-        helper = jnp.where(has_right, p + 1, p - 1)
-        lead = min(2, nch)
-        for c in range(lead):
-            wait_own_kv(c)
-            kv_copy(p, c, helper, own_send.at[0, c]).start()
-        start_x()
-        wait_x(1)
-        dq_copy(helper).start()
-        for c in range(lead, nch):
-            wait_own_kv(c)
-            kv_copy(p, c, helper, own_send.at[0, c]).start()
-        for cp in text_copies:
-            cp.wait()
-        wait_x(0)
-        for c in range(nch):
-            cross_chunk(c)
-            if c > 0:
-                send_out(outc, co, c - 1, c_send, c_recv, c_loc)
-        send_out(outc, co, nch - 1, c_send, c_recv, c_loc)
-        wait_x(2)
-        wait_x(3)
-        states = [first(j) for j in range(heads)]
-        for c in range(nch):
-            for cp in neighbour(c, helper):
-                cp.wait_recv()
-            for i in range(cheads):
-                top, total, mix = states[c * cheads + i]
-                cols = slice(i * HD, (i + 1) * HD)
-                lse = stat_in[c, :, i : i + 1]
-                new_top = jnp.maximum(top, lse)
-                mine = jnp.exp(top - new_top)
-                theirs = jnp.exp(lse - new_top)
-                mix = mix * mine + part_in[c, :, cols].astype(jnp.float32) * theirs
-                outs[c, :, cols] = (mix / (total * mine + theirs)).astype(jnp.bfloat16)
-            send_out(outs, so, c, o_send, o_recv, o_loc)
-        for c in range(nch):
-            kv_copy(p, c, helper, own_send.at[0, c]).wait_send()
-        dq_copy(helper).wait_send()
-
-    def helper_program():
-        end = jnp.where(p < across, p - 1, p + 1)
-        far = n_patch - 1 - end
-        for c in range(nch):
-            wait_own_kv(c)
-            kv_copy(p, c, across, own_send.at[0, c]).start()
-
-        start_x()
-
-        def pass_on(c):
-            kv_copy(end, c, across, fwd_send.at[0, c]).wait_recv()
-            kv_copy(end, c, across, fwd_send.at[0, c]).start()
-
-        pass_on(0)
-        for cp in text_copies:
-            cp.wait()
-        wait_x(0)
-        for c in range(nch):
-            cross_chunk(c)
-            if c > 0:
-                send_out(outc, co, c - 1, c_send, c_recv, c_loc)
-            if c + 1 < nch:
-                pass_on(c + 1)
-        send_out(outc, co, nch - 1, c_send, c_recv, c_loc)
-        for a in range(1, 4):
-            wait_x(a)
-        dq_copy(end).wait_recv()
-
-        def both(j):
-            return jnp.concatenate([query(j), dq[:, pl.ds(j * HD, HD)]], axis=0)
-
-        states = []
-        for j in range(heads):
-            mine = weigh(
-                query(j),
-                jnp.concatenate([fresh_rows(0, j), kv_rows(0, j, end)], axis=0),
-                jnp.concatenate([fresh_rows(1, j), kv_rows(1, j, end)], axis=0),
-            )
-            theirs = weigh(dq[:, pl.ds(j * HD, HD)], kv_rows(0, j, p), kv_rows(1, j, p))
-            states.append([jnp.concatenate(pair, axis=0) for pair in zip(mine, theirs)])
-        for c in range(nch):
-            kv_copy(across, c, p, own_send.at[0, c]).wait_recv()
-        for c in range(nch):
-            kv_copy(far, c, p, own_send.at[0, c]).wait_recv()
-            stat = jnp.zeros((prows, HD), jnp.float32)
-            for i in range(cheads):
-                j = c * cheads + i
-                top, total, mix = absorb_rows(
-                    states[j], both(j), kv_rows(0, j, across, far), kv_rows(1, j, across, far)
-                )
-                mixed = (mix / total).astype(jnp.bfloat16)
-                lse = top[prows:] + jnp.log(total[prows:])
-                stat = jnp.where(lanes == i, lse, stat)
-                part_out[c, :, i * HD : (i + 1) * HD] = mixed[prows:]
-                outs[c, :, i * HD : (i + 1) * HD] = mixed[:prows]
-                if i == early - 1:
-                    neighbour(c, end)[0].start()
-            stat_out[c] = stat
-            for cp in neighbour(c, end)[1:]:
-                cp.start()
-            send_out(outs, so, c, o_send, o_recv, o_loc)
-        for c in range(nch):
-            kv_copy(p, c, across, own_send.at[0, c]).wait_send()
-            kv_copy(end, c, across, fwd_send.at[0, c]).wait_send()
-            for cp in neighbour(c, end):
-                cp.wait_send()
-
-    if n_patch == 4:
-        pl.when(is_end)(end_program)
-        pl.when(jnp.logical_not(is_end))(helper_program)
-    else:
-        line_program()
+    line_program()
 
     for a in range(4):
         for k in range(1, n_head):
@@ -456,33 +309,7 @@
             local_out(src_ref, dst, c, loc).wait()
 
 
-def store_kernel(a, b, so, co, sem):
-    copies = [
-        pltpu.make_async_copy(a, so, sem.at[0]),
-        pltpu.make_async_copy(b, co, sem.at[1]),
-    ]
-    for cp in copies:
-        cp.start()
-    for cp in copies:
-        cp.wait()
-
-
-def store(a, b):
-    return pl.pallas_call(
-        store_kernel,
-        out_shape=(
-            jax.ShapeDtypeStruct(a.shape, a.dtype),
-            jax.ShapeDtypeStruct(b.shape, b.dtype),
-        ),
-        in_specs=[pl.BlockSpec(memory_space=pltpu.VMEM)] * 2,
-        out_specs=(pl.BlockSpec(memory_space=pltpu.HBM),) * 2,
-        scratch_shapes=[pltpu.SemaphoreType.DMA((2,))],
-        compiler_params=pltpu.CompilerParams(vmem_limit_bytes=1024 * 1024),
-        name="store_outputs",
-    )(a, b)
-
-
-def per_device(n_patch, n_head, *args):
+def line_attention(n_patch, n_head, *args):
     fq, fk, fv, sk, sv, cq, tk, tv, mask = args
     rows = fq.shape[1]
     prows = rows * n_head
@@ -496,7 +323,7 @@
     dma = pltpu.SemaphoreType.DMA
     bf16 = jnp.bfloat16
     mixed = pl.pallas_call(
-        functools.partial(kernel, n_patch, n_head, nch),
+        functools.partial(line_kernel, n_patch, n_head, nch),
         out_shape=(
             pltpu.VMEM(fq.shape, bf16),
             pltpu.VMEM(cq.shape, bf16),
@@ -525,19 +352,326 @@
             dma((nch, peers)),
             dma((nch, peers)),
             dma((nch,)),
-            pltpu.VMEM((prows, hcols), bf16),
-            pltpu.VMEM((nch, prows, ccols), bf16),
-            pltpu.VMEM((nch, prows, ccols), bf16),
-            pltpu.VMEM((nch, prows, HD), jnp.float32),
-            pltpu.VMEM((nch, prows, HD), jnp.float32),
-            dma((2,)),
-            dma((nch, 3)),
-            dma((nch, 3)),
         ],
         compiler_params=pltpu.CompilerParams(collective_id=0, has_side_effects=True),
         name="displaced_attention",
     )(*args)
-    return store(*mixed)
+    return mixed
+
+
+END, ACROSS, FAR, OWN = range(4)
+CQ, FQ, FK, FV = range(4)
+
+
+def quad_kernel(
+    n_head, nch,
+    fq, fk, fv, sk, sv, cq, tk, tv, mask,
+    so, co,
+    fx, kv, tx, mk, dq, part, stat, outs, oute, outc,
+    x_in, t_in, own_in, end_in, far_in, across_in, q_in, part_in, out_in, sent,
+):
+    p = lax.axis_index("patch")
+    h = lax.axis_index("head")
+    rows = fq.shape[1]
+    prows = rows * n_head
+    hcols = sk.shape[2]
+    heads = hcols // HD
+    cheads = heads // nch
+    scale = 1.0 / math.sqrt(HD)
+    fresh = (cq, fq, fk, fv)
+    x_sem = (0, 1, 2, 2)
+    across = 3 - p
+    is_end = (p == 0) | (p == 3)
+    inner = jnp.where(p < 2, 1, 2)
+    outer = jnp.where(p < 2, 0, 3)
+    my_rows = pl.ds(pl.multiple_of(h * rows, rows), rows)
+
+    def head_cols(who):
+        return pl.ds(pl.multiple_of(who * hcols, hcols), hcols)
+
+    def cols(c):
+        return pl.ds(c * cheads * HD, cheads * HD)
+
+    def own_copy(a):
+        return pltpu.make_async_copy(
+            fresh[a].at[0, :, head_cols(h)], fx.at[a, my_rows, :], x_in.at[x_sem[a]]
+        )
+
+    def remote(src, dst, send, recv, **to):
+        return pltpu.make_async_remote_copy(
+            src_ref=src, dst_ref=dst, send_sem=send, recv_sem=recv,
+            device_id=to, device_id_type=MESH,
+        )
+
+    def wait_bytes(ref, sem):
+        pltpu.make_async_copy(ref, ref, sem).wait()
+
+    def load_text():
+        pltpu.make_async_copy(mask, mk, t_in.at[0]).start()
+        pltpu.make_async_copy(tk.at[0], tx.at[0], t_in.at[1]).start()
+        pltpu.make_async_copy(tv.at[0], tx.at[1], t_in.at[1]).start()
+
+    barrier = pltpu.get_barrier_semaphore()
+    for k in range(1, n_head):
+        pl.semaphore_signal(
+            barrier, inc=1, device_id={"head": lax.rem(h + k, n_head)}, device_id_type=MESH
+        )
+
+    @pl.when(is_end)
+    def _():
+        pl.semaphore_signal(barrier, inc=1, device_id={"patch": inner}, device_id_type=MESH)
+
+    @pl.when(jnp.logical_not(is_end))
+    def _():
+        pl.semaphore_signal(barrier, inc=1, device_id={"patch": across}, device_id_type=MESH)
+        pl.semaphore_signal(barrier, inc=1, device_id={"patch": outer}, device_id_type=MESH)
+        for i, ref in enumerate((sk, sv)):
+            pltpu.make_async_copy(ref.at[0], kv.at[OWN, i], own_in.at[0]).start()
+
+    for a in range(4):
+        own_copy(a).start()
+    load_text()
+    pl.semaphore_wait(barrier, n_head - 1 + jnp.where(is_end, 1, 2))
+
+    def send_x(a):
+        for k in range(1, n_head):
+            peer = lax.rem(h + k, n_head)
+            remote(
+                fresh[a].at[0, :, head_cols(peer)], fx.at[a, my_rows, :],
+                sent.at[0], x_in.at[x_sem[a]], head=peer,
+            ).start()
+
+    def scores_of(q, keys):
+        return dot_nt(q, keys) * scale
+
+    def mix_of(weights, values):
+        wide = jnp.concatenate([values, jnp.ones_like(values)], axis=1)
+        mixed = jnp.dot(
+            weights.astype(jnp.bfloat16), wide, preferred_element_type=jnp.float32
+        )
+        return mixed[:, :HD], mixed[:, HD:]
+
+    def cross_heads(first, last):
+        usable = mk[...] > 0
+        for j in range(first, last):
+            at = slice(j * HD, (j + 1) * HD)
+            scores = jnp.where(usable, scores_of(fx[CQ, :, at], tx[0, :, at]), -jnp.inf)
+            weights = jnp.exp(scores - jnp.max(scores, axis=-1, keepdims=True))
+            total = jnp.sum(weights, axis=-1, keepdims=True)
+            mix = jnp.dot(
+                weights.astype(jnp.bfloat16), tx[1, :, at], preferred_element_type=jnp.float32
+            )
+            outc[:, at] = (mix / total).astype(jnp.bfloat16)
+
+    def send_out(src, dst, at, size, send, recv):
+        dst_at = dst.at[0, :, pl.ds(pl.multiple_of(h * hcols + at, HD), size)]
+        for k in range(1, n_head):
+            peer = lax.rem(h + k, n_head)
+            remote(
+                src.at[pl.ds(pl.multiple_of(peer * rows, rows), rows), pl.ds(at, size)],
+                dst_at, send, recv, head=peer,
+            ).start()
+        pltpu.make_async_copy(src.at[my_rows, pl.ds(at, size)], dst_at, recv).start()
+
+    def send_cross():
+        send_out(outc, co, 0, hcols, sent.at[1], out_in.at[1])
+
+    def wait_text():
+        wait_bytes(mk, t_in.at[0])
+        wait_bytes(tx, t_in.at[1])
+
+    def end_program():
+        def send_kv(c):
+            for i, ref in enumerate((sk, sv)):
+                remote(
+                    ref.at[0, :, cols(c)], kv.at[END, i, :, cols(c)],
+                    sent.at[2], end_in.at[c], patch=inner,
+                ).start()
+
+        lead = (nch + 1) // 2
+        send_x(FQ)
+        send_kv(0)
+        send_x(FK)
+        send_x(FV)
+        send_x(CQ)
+        for c in range(1, lead):
+            send_kv(c)
+        wait_bytes(fx.at[FQ], x_in.at[1])
+        remote(fx.at[FQ], dq, sent.at[3], q_in.at[0], patch=inner).start()
+        for c in range(lead, nch):
+            send_kv(c)
+        wait_bytes(fx.at[pl.ds(FK, 2)], x_in.at[2])
+        lanes = lax.broadcasted_iota(jnp.int32, (prows, HD), 1)
+        lse = jnp.zeros((prows, HD), jnp.float32)
+        for j in range(heads):
+            at = slice(j * HD, (j + 1) * HD)
+            scores = scores_of(fx[FQ, :, at], fx[FK, :, at])
+            top = jnp.max(scores, axis=-1, keepdims=True)
+            mix, total = mix_of(jnp.exp(scores - top), fx[FV, :, at])
+            outs[:, at] = (mix / total).astype(jnp.bfloat16)
+            lse = jnp.where(lanes == j, top + jnp.log(total), lse)
+        stat[1] = lse
+        remote(outs, part, sent.at[4], part_in.at[0], patch=inner).start()
+        remote(stat.at[1], stat.at[0], sent.at[5], part_in.at[1], patch=inner).start()
+        wait_text()
+        wait_bytes(fx.at[CQ], x_in.at[0])
+        cross_heads(0, heads)
+        send_cross()
+        wait_bytes(kv.at[END], sent.at[2])
+        wait_bytes(dq, sent.at[3])
+        wait_bytes(part, sent.at[4])
+        wait_bytes(stat.at[0], sent.at[5])
+
+    def middle_program():
+        for i, ref in enumerate((sk, sv)):
+            remote(
+                ref.at[0], kv.at[ACROSS, i], sent.at[2], across_in.at[0], patch=across
+            ).start()
+        for a in (CQ, FQ, FK, FV):
+            send_x(a)
+
+        def pass_on(c):
+            src = kv.at[END, :, :, cols(c)]
+            wait_bytes(src, end_in.at[c])
+            remote(
+                src, kv.at[FAR, :, :, cols(c)], sent.at[3], far_in.at[c], patch=across
+            ).start()
+
+        pass_on(0)
+        wait_text()
+        wait_bytes(fx.at[CQ], x_in.at[0])
+        half = heads // 2
+        cross_heads(0, half)
+        if nch > 1:
+            pass_on(1)
+        cross_heads(half, heads)
+        send_cross()
+        for c in range(2, nch):
+            pass_on(c)
+        wait_bytes(fx.at[FQ], x_in.at[1])
+        wait_bytes(fx.at[pl.ds(FK, 2)], x_in.at[2])
+        wait_bytes(kv.at[OWN], own_in.at[0])
+        wait_bytes(kv.at[ACROSS], across_in.at[0])
+        wait_bytes(dq, q_in.at[0])
+        wait_bytes(part, part_in.at[0])
+        wait_bytes(stat.at[0], part_in.at[1])
+        for c in range(nch):
+            wait_bytes(kv.at[FAR, :, :, cols(c)], far_in.at[c])
+            for j in range(c * cheads, (c + 1) * cheads):
+                at = slice(j * HD, (j + 1) * HD)
+                shared = [[kv[s, i, :, at] for s in (ACROSS, FAR)] for i in range(2)]
+                keys = jnp.concatenate([kv[OWN, 0, :, at]] + shared[0], axis=0)
+                values = jnp.concatenate([kv[OWN, 1, :, at]] + shared[1], axis=0)
+                scores = scores_of(dq[:, at], keys)
+                lse = stat[0, :, j : j + 1]
+                top = jnp.maximum(jnp.max(scores, axis=-1, keepdims=True), lse)
+                mix, total = mix_of(jnp.exp(scores - top), values)
+                theirs = jnp.exp(lse - top)
+                mix = mix + part[:, at].astype(jnp.float32) * theirs
+                oute[:, at] = (mix / (total + theirs)).astype(jnp.bfloat16)
+                keys = jnp.concatenate([fx[FK, :, at], kv[END, 0, :, at]] + shared[0], axis=0)
+                values = jnp.concatenate([fx[FV, :, at], kv[END, 1, :, at]] + shared[1], axis=0)
+                scores = scores_of(fx[FQ, :, at], keys)
+                top = jnp.max(scores, axis=-1, keepdims=True)
+                mix, total = mix_of(jnp.exp(scores - top), values)
+                outs[:, at] = (mix / total).astype(jnp.bfloat16)
+            size = cheads * HD
+            first = c * size
+            dst = so.at[0, :, pl.ds(pl.multiple_of(h * hcols + first, HD), size)]
+            for k in range(n_head - 1, -1, -1):
+                to = lax.rem(h + k, n_head)
+                remote(
+                    oute.at[pl.ds(pl.multiple_of(to * rows, rows), rows), pl.ds(first, size)],
+                    dst, sent.at[4], out_in.at[0], patch=outer, head=to,
+                ).start()
+            send_out(outs, so, first, size, sent.at[5], out_in.at[0])
+        wait_bytes(kv.at[ACROSS], sent.at[2])
+        wait_bytes(kv.at[FAR], sent.at[3])
+        wait_bytes(oute, sent.at[4])
+        if n_head > 1:
+            wait_bytes(outs.at[pl.ds(0, rows * (n_head - 1)), :], sent.at[5])
+
+    pl.when(is_end)(end_program)
+    pl.when(jnp.logical_not(is_end))(middle_program)
+    if n_head > 1:
+        wait_bytes(fx.at[:, pl.ds(0, rows * (n_head - 1)), :], sent.at[0])
+        wait_bytes(outc.at[pl.ds(0, rows * (n_head - 1)), :], sent.at[1])
+    wait_bytes(co, out_in.at[1])
+    wait_bytes(so, out_in.at[0])
+
+
+def quad_attention(n_head, *args):
+    fq, fk, fv, sk, sv, cq, tk, tv, mask = args
+    prows = fq.shape[1] * n_head
+    hcols = sk.shape[2]
+    heads = hcols // HD
+    nch = next(n for n in (5, 4, 3, 2, 1) if heads % n == 0)
+    txt = tk.shape[1]
+    dma = pltpu.SemaphoreType.DMA
+    bf16 = jnp.bfloat16
+    patch = pltpu.VMEM((prows, hcols), bf16)
+    return pl.pallas_call(
+        functools.partial(quad_kernel, n_head, nch),
+        out_shape=(pltpu.VMEM(fq.shape, bf16), pltpu.VMEM(cq.shape, bf16)),
+        in_specs=[pl.BlockSpec(memory_space=pl.ANY)] * 9,
+        out_specs=(pl.BlockSpec(memory_space=pltpu.VMEM),) * 2,
+        scratch_shapes=[
+            pltpu.VMEM((4, prows, hcols), bf16),
+            pltpu.VMEM((4, 2, prows, hcols), bf16),
+            pltpu.VMEM((2, txt, hcols), bf16),
+            pltpu.VMEM((1, txt), jnp.int32),
+            patch,
+            patch,
+            pltpu.VMEM((2, prows, HD), jnp.float32),
+            patch,
+            patch,
+            patch,
+            dma((3,)),
+            dma((2,)),
+            dma((1,)),
+            dma((nch,)),
+            dma((nch,)),
+            dma((1,)),
+            dma((1,)),
+            dma((2,)),
+            dma((2,)),
+            dma((6,)),
+        ],
+        compiler_params=pltpu.CompilerParams(collective_id=0, has_side_effects=True),
+        name="displaced_attention",
+    )(*args)
+
+
+def store_kernel(a, b, so, co, sem):
+    copies = [
+        pltpu.make_async_copy(a, so, sem.at[0]),
+        pltpu.make_async_copy(b, co, sem.at[1]),
+    ]
+    for cp in copies:
+        cp.start()
+    for cp in copies:
+        cp.wait()
+
+
+def store(a, b):
+    return pl.pallas_call(
+        store_kernel,
+        out_shape=(
+            jax.ShapeDtypeStruct(a.shape, a.dtype),
+            jax.ShapeDtypeStruct(b.shape, b.dtype),
+        ),
+        in_specs=[pl.BlockSpec(memory_space=pltpu.VMEM)] * 2,
+        out_specs=(pl.BlockSpec(memory_space=pltpu.HBM),) * 2,
+        scratch_shapes=[pltpu.SemaphoreType.DMA((2,))],
+        compiler_params=pltpu.CompilerParams(vmem_limit_bytes=1024 * 1024),
+        name="store_outputs",
+    )(a, b)
+
+
+def per_device(n_patch, n_head, *args):
+    if n_patch == 4:
+        return store(*quad_attention(n_head, *args))
+    return store(*line_attention(n_patch, n_head, *args))
 
 
 def solution(mesh):

time: 31.2 us -> 30.3 us (0.971)
  Pallas kernels: 30.4 us -> 29.5 us
    pallas_call x1, Pallas kernels: 29.7 us -> 28.7 us  [quad_attention(): pl.pallas_call(functools.partial(quad_kernel, n_head, nch), out_shape=(pl...]
where the time goes in v1:
time: 30.3 us; the launch traced here: 30.1 us
  Pallas kernels  29.5 us (97%)
  between operations  0.64 us (2%)
    pallas_call x1, Pallas kernels, quad_attention(): pl.pallas_call(functools.partial(quad_kernel, n_head, nch), out_shape=(pl...  28.7 us
    pallas_call x1, Pallas kernels, store(): pl.pallas_call(store_kernel, out_shape=(jax.ShapeDtypeStruct(a.shape, a.d...  0.74 us

profile of v1, /device:TPU:0, one launch (start us, length us, event | category | flops | bytes accessed | tf_op | source)
XLA Modules:
  0.0 30.1 jit_solution(690110367908069941)
XLA Ops:
  0.6 28.7 %displaced_attention.1 = (bf16[1,32,2560]{2,1,0:T(8,128)(2,1)S(1)}, bf16[1,32,2560]{2,1,0:T(8,128)(2,1)S(1)}) custom-call(bf16[1,32,2560]{2,1,0:T(8,128)(2,1)} %fq.1, bf16[1,32,2560]{2,1,0:T(8,128)(2,1)} %fk.1, bf16[1,32,2560]{2,1,0:T(8,128)(2,1)} %fv.1, bf16[1,64,1280]{2,1,0:T(8,128)(2,1)} %sk.1, bf16[1,64,1280]{2,1,0:T(8,128)(2,1)} %sv.1, ...), custom_call_target="tpu_custom_call" | custom-call | tf_op jit(solution)/shard_map/displaced_attention/pallas_call | solution.py:613
  29.4 0.7 %store_outputs.1 = (bf16[1,32,2560]{2,1,0:T(8,128)(2,1)}, bf16[1,32,2560]{2,1,0:T(8,128)(2,1)}) custom-call(bf16[1,32,2560]{2,1,0:T(8,128)(2,1)S(1)} %get-tuple-element.4.a, bf16[1,32,2560]{2,1,0:T(8,128)(2,1)S(1)} %get-tuple-element.5.b), custom_call_target="tpu_custom_call" | custom-call | tf_op jit(solution)/shard_map/store_outputs/pallas_call | solution.py:657

commit v2 on v1

--- a/solution.py
+++ b/solution.py
@@ -361,10 +361,17 @@
 
 END, ACROSS, FAR, OWN = range(4)
 CQ, FQ, FK, FV = range(4)
+DIRECT = 3
+
+
+def chunk_sizes(heads):
+    size = max(1, heads // 5)
+    whole = (heads - 1) // size
+    return [size] * whole + [1] * (heads - whole * size)
 
 
 def quad_kernel(
-    n_head, nch,
+    n_head, direct,
     fq, fk, fv, sk, sv, cq, tk, tv, mask,
     so, co,
     fx, kv, tx, mk, dq, part, stat, outs, oute, outc,
@@ -376,7 +383,11 @@
     prows = rows * n_head
     hcols = sk.shape[2]
     heads = hcols // HD
-    cheads = heads // nch
+    sizes = chunk_sizes(heads)
+    nch = len(sizes)
+    starts = [sum(sizes[:c]) for c in range(nch + 1)]
+    early = slice(0, starts[direct] * HD)
+    late = slice(starts[direct] * HD, hcols)
     scale = 1.0 / math.sqrt(HD)
     fresh = (cq, fq, fk, fv)
     x_sem = (0, 1, 2, 2)
@@ -390,7 +401,7 @@
         return pl.ds(pl.multiple_of(who * hcols, hcols), hcols)
 
     def cols(c):
-        return pl.ds(c * cheads * HD, cheads * HD)
+        return slice(starts[c] * HD, starts[c + 1] * HD)
 
     def own_copy(a):
         return pltpu.make_async_copy(
@@ -450,6 +461,31 @@
             weights.astype(jnp.bfloat16), wide, preferred_element_type=jnp.float32
         )
         return mixed[:, :HD], mixed[:, HD:]
+
+    def attend_own(c):
+        for j in range(starts[c], starts[c + 1]):
+            at = slice(j * HD, (j + 1) * HD)
+            keys, values = (
+                jnp.concatenate([fx[FK + i, :, at]] + [kv[s, i, :, at] for s in (END, ACROSS, FAR)])
+                for i in range(2)
+            )
+            scores = scores_of(fx[FQ, :, at], keys)
+            mix, total = mix_of(jnp.exp(scores - jnp.max(scores, axis=-1, keepdims=True)), values)
+            outs[:, at] = (mix / total).astype(jnp.bfloat16)
+
+    def attend_end(c):
+        for j in range(starts[c], starts[c + 1]):
+            at = slice(j * HD, (j + 1) * HD)
+            keys, values = (
+                jnp.concatenate([kv[s, i, :, at] for s in (OWN, ACROSS, FAR)]) for i in range(2)
+            )
+            scores = scores_of(dq[:, at], keys)
+            lse = stat[0, :, j : j + 1]
+            top = jnp.maximum(jnp.max(scores, axis=-1, keepdims=True), lse)
+            mix, total = mix_of(jnp.exp(scores - top), values)
+            theirs = jnp.exp(lse - top)
+            mix = mix + part[:, at].astype(jnp.float32) * theirs
+            oute[:, at] = (mix / (total + theirs)).astype(jnp.bfloat16)
 
     def cross_heads(first, last):
         usable = mk[...] > 0
@@ -463,18 +499,24 @@
             )
             outc[:, at] = (mix / total).astype(jnp.bfloat16)
 
-    def send_out(src, dst, at, size, send, recv):
-        dst_at = dst.at[0, :, pl.ds(pl.multiple_of(h * hcols + at, HD), size)]
+    def out_at(dst, at):
+        return dst.at[0, :, pl.ds(pl.multiple_of(h * hcols + at.start, HD), at.stop - at.start)]
+
+    def rows_of(src, who, at):
+        return src.at[pl.ds(pl.multiple_of(who * rows, rows), rows), at]
+
+    def send_out(src, dst, at, send, recv):
         for k in range(1, n_head):
             peer = lax.rem(h + k, n_head)
-            remote(
-                src.at[pl.ds(pl.multiple_of(peer * rows, rows), rows), pl.ds(at, size)],
-                dst_at, send, recv, head=peer,
-            ).start()
-        pltpu.make_async_copy(src.at[my_rows, pl.ds(at, size)], dst_at, recv).start()
+            remote(rows_of(src, peer, at), out_at(dst, at), send, recv, head=peer).start()
+        pltpu.make_async_copy(rows_of(src, h, at), out_at(dst, at), recv).start()
+
+    def wait_peers(src, at, send):
+        if n_head > 1:
+            wait_bytes(src.at[pl.ds(0, rows * (n_head - 1)), at], send)
 
     def send_cross():
-        send_out(outc, co, 0, hcols, sent.at[1], out_in.at[1])
+        send_out(outc, co, slice(0, hcols), sent.at[1], out_in.at[1])
 
     def wait_text():
         wait_bytes(mk, t_in.at[0])
@@ -497,13 +539,15 @@
         for c in range(1, lead):
             send_kv(c)
         wait_bytes(fx.at[FQ], x_in.at[1])
-        remote(fx.at[FQ], dq, sent.at[3], q_in.at[0], patch=inner).start()
+        remote(
+            fx.at[FQ, :, late], dq.at[:, late], sent.at[3], q_in.at[0], patch=inner
+        ).start()
         for c in range(lead, nch):
             send_kv(c)
         wait_bytes(fx.at[pl.ds(FK, 2)], x_in.at[2])
         lanes = lax.broadcasted_iota(jnp.int32, (prows, HD), 1)
         lse = jnp.zeros((prows, HD), jnp.float32)
-        for j in range(heads):
+        for j in range(starts[direct], heads):
             at = slice(j * HD, (j + 1) * HD)
             scores = scores_of(fx[FQ, :, at], fx[FK, :, at])
             top = jnp.max(scores, axis=-1, keepdims=True)
@@ -511,91 +555,102 @@
             outs[:, at] = (mix / total).astype(jnp.bfloat16)
             lse = jnp.where(lanes == j, top + jnp.log(total), lse)
         stat[1] = lse
-        remote(outs, part, sent.at[4], part_in.at[0], patch=inner).start()
+        remote(
+            outs.at[:, late], part.at[:, late], sent.at[4], part_in.at[0], patch=inner
+        ).start()
         remote(stat.at[1], stat.at[0], sent.at[5], part_in.at[1], patch=inner).start()
         wait_text()
         wait_bytes(fx.at[CQ], x_in.at[0])
         cross_heads(0, heads)
         send_cross()
+        for c in range(direct):
+            wait_bytes(kv.at[pl.ds(END, 3), :, :, cols(c)], far_in.at[c])
+            attend_own(c)
+            send_out(outs, so, cols(c), sent.at[6], out_in.at[0])
         wait_bytes(kv.at[END], sent.at[2])
-        wait_bytes(dq, sent.at[3])
-        wait_bytes(part, sent.at[4])
+        wait_bytes(dq.at[:, late], sent.at[3])
+        wait_bytes(part.at[:, late], sent.at[4])
         wait_bytes(stat.at[0], sent.at[5])
+        if direct:
+            wait_peers(outs, early, sent.at[6])
 
     def middle_program():
-        for i, ref in enumerate((sk, sv)):
+        def send_own(at, recv):
+            for i, ref in enumerate((sk, sv)):
+                remote(
+                    ref.at[0, :, at], kv.at[ACROSS, i, :, at], sent.at[2], recv, patch=across
+                ).start()
+
+        def pass_out(src, slot, c):
             remote(
-                ref.at[0], kv.at[ACROSS, i], sent.at[2], across_in.at[0], patch=across
+                src, kv.at[slot, :, :, cols(c)], sent.at[6], far_in.at[c], patch=outer
             ).start()
-        for a in (CQ, FQ, FK, FV):
-            send_x(a)
-
-        def pass_on(c):
+
+        def pass_across(c):
             src = kv.at[END, :, :, cols(c)]
             wait_bytes(src, end_in.at[c])
             remote(
                 src, kv.at[FAR, :, :, cols(c)], sent.at[3], far_in.at[c], patch=across
             ).start()
 
-        pass_on(0)
+        if direct:
+            send_own(early, across_in.at[0])
+        send_own(late, across_in.at[1])
+        for a in (CQ, FQ, FK, FV):
+            send_x(a)
+        wait_bytes(kv.at[OWN], own_in.at[0])
+        for c in range(direct):
+            pass_out(kv.at[OWN, :, :, cols(c)], END, c)
+        pass_across(0)
         wait_text()
         wait_bytes(fx.at[CQ], x_in.at[0])
         half = heads // 2
         cross_heads(0, half)
+        if direct:
+            wait_bytes(kv.at[ACROSS, :, :, early], across_in.at[0])
+        for c in range(direct):
+            pass_out(kv.at[ACROSS, :, :, cols(c)], ACROSS, c)
         if nch > 1:
-            pass_on(1)
+            pass_across(1)
         cross_heads(half, heads)
         send_cross()
         for c in range(2, nch):
-            pass_on(c)
+            pass_across(c)
         wait_bytes(fx.at[FQ], x_in.at[1])
         wait_bytes(fx.at[pl.ds(FK, 2)], x_in.at[2])
-        wait_bytes(kv.at[OWN], own_in.at[0])
-        wait_bytes(kv.at[ACROSS], across_in.at[0])
-        wait_bytes(dq, q_in.at[0])
-        wait_bytes(part, part_in.at[0])
+        wait_bytes(kv.at[ACROSS, :, :, late], across_in.at[1])
+        for c in range(direct):
+            far = kv.at[FAR, :, :, cols(c)]
+            wait_bytes(far, far_in.at[c])
+            pass_out(far, FAR, c)
+            attend_own(c)
+            send_out(outs, so, cols(c), sent.at[5], out_in.at[0])
+        wait_bytes(dq.at[:, late], q_in.at[0])
+        wait_bytes(part.at[:, late], part_in.at[0])
         wait_bytes(stat.at[0], part_in.at[1])
-        for c in range(nch):
+        for c in range(direct, nch):
             wait_bytes(kv.at[FAR, :, :, cols(c)], far_in.at[c])
-            for j in range(c * cheads, (c + 1) * cheads):
-                at = slice(j * HD, (j + 1) * HD)
-                shared = [[kv[s, i, :, at] for s in (ACROSS, FAR)] for i in range(2)]
-                keys = jnp.concatenate([kv[OWN, 0, :, at]] + shared[0], axis=0)
-                values = jnp.concatenate([kv[OWN, 1, :, at]] + shared[1], axis=0)
-                scores = scores_of(dq[:, at], keys)
-                lse = stat[0, :, j : j + 1]
-                top = jnp.maximum(jnp.max(scores, axis=-1, keepdims=True), lse)
-                mix, total = mix_of(jnp.exp(scores - top), values)
-                theirs = jnp.exp(lse - top)
-                mix = mix + part[:, at].astype(jnp.float32) * theirs
-                oute[:, at] = (mix / (total + theirs)).astype(jnp.bfloat16)
-                keys = jnp.concatenate([fx[FK, :, at], kv[END, 0, :, at]] + shared[0], axis=0)
-                values = jnp.concatenate([fx[FV, :, at], kv[END, 1, :, at]] + shared[1], axis=0)
-                scores = scores_of(fx[FQ, :, at], keys)
-                top = jnp.max(scores, axis=-1, keepdims=True)
-                mix, total = mix_of(jnp.exp(scores - top), values)
-                outs[:, at] = (mix / total).astype(jnp.bfloat16)
-            size = cheads * HD
-            first = c * size
-            dst = so.at[0, :, pl.ds(pl.multiple_of(h * hcols + first, HD), size)]
+            attend_end(c)
             for k in range(n_head - 1, -1, -1):
                 to = lax.rem(h + k, n_head)
                 remote(
-                    oute.at[pl.ds(pl.multiple_of(to * rows, rows), rows), pl.ds(first, size)],
-                    dst, sent.at[4], out_in.at[0], patch=outer, head=to,
+                    rows_of(oute, to, cols(c)), out_at(so, cols(c)),
+                    sent.at[4], out_in.at[0], patch=outer, head=to,
                 ).start()
-            send_out(outs, so, first, size, sent.at[5], out_in.at[0])
+            attend_own(c)
+            send_out(outs, so, cols(c), sent.at[5], out_in.at[0])
         wait_bytes(kv.at[ACROSS], sent.at[2])
         wait_bytes(kv.at[FAR], sent.at[3])
-        wait_bytes(oute, sent.at[4])
-        if n_head > 1:
-            wait_bytes(outs.at[pl.ds(0, rows * (n_head - 1)), :], sent.at[5])
+        wait_bytes(oute.at[:, late], sent.at[4])
+        wait_peers(outs, slice(0, hcols), sent.at[5])
+        if direct:
+            wait_bytes(kv.at[pl.ds(END, 3), :, :, early], sent.at[6])
 
     pl.when(is_end)(end_program)
     pl.when(jnp.logical_not(is_end))(middle_program)
     if n_head > 1:
         wait_bytes(fx.at[:, pl.ds(0, rows * (n_head - 1)), :], sent.at[0])
-        wait_bytes(outc.at[pl.ds(0, rows * (n_head - 1)), :], sent.at[1])
+    wait_peers(outc, slice(0, hcols), sent.at[1])
     wait_bytes(co, out_in.at[1])
     wait_bytes(so, out_in.at[0])
 
@@ -605,13 +660,14 @@
     prows = fq.shape[1] * n_head
     hcols = sk.shape[2]
     heads = hcols // HD
-    nch = next(n for n in (5, 4, 3, 2, 1) if heads % n == 0)
+    nch = len(chunk_sizes(heads))
+    direct = min(DIRECT, nch - 1)
     txt = tk.shape[1]
     dma = pltpu.SemaphoreType.DMA
     bf16 = jnp.bfloat16
     patch = pltpu.VMEM((prows, hcols), bf16)
     return pl.pallas_call(
-        functools.partial(quad_kernel, n_head, nch),
+        functools.partial(quad_kernel, n_head, direct),
         out_shape=(pltpu.VMEM(fq.shape, bf16), pltpu.VMEM(cq.shape, bf16)),
         in_specs=[pl.BlockSpec(memory_space=pl.ANY)] * 9,
         out_specs=(pl.BlockSpec(memory_space=pltpu.VMEM),) * 2,
@@ -631,11 +687,11 @@
             dma((1,)),
             dma((nch,)),
             dma((nch,)),
-            dma((1,)),
+            dma((2,)),
             dma((1,)),
             dma((2,)),
             dma((2,)),
-            dma((6,)),
+            dma((7,)),
         ],
         compiler_params=pltpu.CompilerParams(collective_id=0, has_side_effects=True),
         name="displaced_attention",

time: 30.3 us -> 27.2 us (0.90)
  Pallas kernels: 29.5 us -> 26.4 us
    pallas_call x1, Pallas kernels: 28.7 us -> 25.6 us  [quad_attention(): pl.pallas_call(functools.partial(quad_kernel, n_head, direct), out_shape=...]
where the time goes in v2:
time: 27.2 us; the launch traced here: 27 us
  Pallas kernels  26.4 us (97%)
  between operations  0.64 us (2%)
    pallas_call x1, Pallas kernels, quad_attention(): pl.pallas_call(functools.partial(quad_kernel, n_head, direct), out_shape=...  25.6 us
    pallas_call x1, Pallas kernels, store(): pl.pallas_call(store_kernel, out_shape=(jax.ShapeDtypeStruct(a.shape, a.d...  0.74 us

profile of v2, /device:TPU:0, one launch (start us, length us, event | category | flops | bytes accessed | tf_op | source)
XLA Modules:
  0.0 27.0 jit_solution(50841432642586537)
XLA Ops:
  0.6 25.6 %displaced_attention.1 = (bf16[1,32,2560]{2,1,0:T(8,128)(2,1)S(1)}, bf16[1,32,2560]{2,1,0:T(8,128)(2,1)S(1)}) custom-call(bf16[1,32,2560]{2,1,0:T(8,128)(2,1)} %fq.1, bf16[1,32,2560]{2,1,0:T(8,128)(2,1)} %fk.1, bf16[1,32,2560]{2,1,0:T(8,128)(2,1)} %fv.1, bf16[1,64,1280]{2,1,0:T(8,128)(2,1)} %sk.1, bf16[1,64,1280]{2,1,0:T(8,128)(2,1)} %sv.1, ...), custom_call_target="tpu_custom_call" | custom-call | tf_op jit(solution)/shard_map/displaced_attention/pallas_call | solution.py:669
  26.3 0.7 %store_outputs.1 = (bf16[1,32,2560]{2,1,0:T(8,128)(2,1)}, bf16[1,32,2560]{2,1,0:T(8,128)(2,1)}) custom-call(bf16[1,32,2560]{2,1,0:T(8,128)(2,1)S(1)} %get-tuple-element.4.a, bf16[1,32,2560]{2,1,0:T(8,128)(2,1)S(1)} %get-tuple-element.5.b), custom_call_target="tpu_custom_call" | custom-call | tf_op jit(solution)/shard_map/store_outputs/pallas_call | solution.py:713

commit v3 on v2

--- a/solution.py
+++ b/solution.py
@@ -361,20 +361,19 @@
 
 END, ACROSS, FAR, OWN = range(4)
 CQ, FQ, FK, FV = range(4)
-DIRECT = 3
-
-
-def chunk_sizes(heads):
-    size = max(1, heads // 5)
-    whole = (heads - 1) // size
-    return [size] * whole + [1] * (heads - whole * size)
+DIRECT = 2
+CROSS = 2
+
+
+def chunk_heads(heads):
+    return max(n for n in range(1, max(1, heads // 5) + 1) if heads % n == 0)
 
 
 def quad_kernel(
     n_head, direct,
     fq, fk, fv, sk, sv, cq, tk, tv, mask,
     so, co,
-    fx, kv, tx, mk, dq, part, stat, outs, oute, outc,
+    fx, kv, tx, mk, dq, part, stat, spread, outs, oute, outc,
     x_in, t_in, own_in, end_in, far_in, across_in, q_in, part_in, out_in, sent,
 ):
     p = lax.axis_index("patch")
@@ -383,11 +382,12 @@
     prows = rows * n_head
     hcols = sk.shape[2]
     heads = hcols // HD
-    sizes = chunk_sizes(heads)
-    nch = len(sizes)
-    starts = [sum(sizes[:c]) for c in range(nch + 1)]
-    early = slice(0, starts[direct] * HD)
-    late = slice(starts[direct] * HD, hcols)
+    cheads = chunk_heads(heads)
+    nch = heads // cheads
+    size = cheads * HD
+    early = pl.ds(0, direct * size)
+    late = pl.ds(direct * size, hcols - direct * size)
+    every = pl.ds(0, hcols)
     scale = 1.0 / math.sqrt(HD)
     fresh = (cq, fq, fk, fv)
     x_sem = (0, 1, 2, 2)
@@ -401,7 +401,10 @@
         return pl.ds(pl.multiple_of(who * hcols, hcols), hcols)
 
     def cols(c):
-        return slice(starts[c] * HD, starts[c + 1] * HD)
+        return pl.ds(c * size if isinstance(c, int) else pl.multiple_of(c * size, size), size)
+
+    def head_at(j):
+        return pl.ds(j * HD if isinstance(j, int) else pl.multiple_of(j * HD, HD), HD)
 
     def own_copy(a):
         return pltpu.make_async_copy(
@@ -462,45 +465,63 @@
         )
         return mixed[:, :HD], mixed[:, HD:]
 
-    def attend_own(c):
-        for j in range(starts[c], starts[c + 1]):
-            at = slice(j * HD, (j + 1) * HD)
-            keys, values = (
-                jnp.concatenate([fx[FK + i, :, at]] + [kv[s, i, :, at] for s in (END, ACROSS, FAR)])
-                for i in range(2)
-            )
-            scores = scores_of(fx[FQ, :, at], keys)
-            mix, total = mix_of(jnp.exp(scores - jnp.max(scores, axis=-1, keepdims=True)), values)
-            outs[:, at] = (mix / total).astype(jnp.bfloat16)
-
-    def attend_end(c):
-        for j in range(starts[c], starts[c + 1]):
-            at = slice(j * HD, (j + 1) * HD)
-            keys, values = (
-                jnp.concatenate([kv[s, i, :, at] for s in (OWN, ACROSS, FAR)]) for i in range(2)
-            )
-            scores = scores_of(dq[:, at], keys)
-            lse = stat[0, :, j : j + 1]
-            top = jnp.maximum(jnp.max(scores, axis=-1, keepdims=True), lse)
-            mix, total = mix_of(jnp.exp(scores - top), values)
-            theirs = jnp.exp(lse - top)
-            mix = mix + part[:, at].astype(jnp.float32) * theirs
-            oute[:, at] = (mix / (total + theirs)).astype(jnp.bfloat16)
+    def own_head(at):
+        keys, values = (
+            jnp.concatenate([fx[FK + i, :, at]] + [kv[s, i, :, at] for s in (END, ACROSS, FAR)])
+            for i in range(2)
+        )
+        scores = scores_of(fx[FQ, :, at], keys)
+        mix, total = mix_of(jnp.exp(scores - jnp.max(scores, axis=-1, keepdims=True)), values)
+        return (mix / total).astype(jnp.bfloat16)
+
+    def end_head(at, lse):
+        keys, values = (
+            jnp.concatenate([kv[s, i, :, at] for s in (OWN, ACROSS, FAR)]) for i in range(2)
+        )
+        scores = scores_of(dq[:, at], keys)
+        top = jnp.maximum(jnp.max(scores, axis=-1, keepdims=True), lse)
+        mix, total = mix_of(jnp.exp(scores - top[:, :1]), values)
+        theirs = jnp.exp(lse - top)
+        mix = mix + part[:, at].astype(jnp.float32) * theirs
+        return (mix / (total + theirs)).astype(jnp.bfloat16)
+
+    def attend(c, both):
+        results = []
+        for i in range(cheads):
+            j = c * cheads + i
+            at = head_at(j)
+            if both:
+                results.append((oute, at, end_head(at, spread[j])))
+            results.append((outs, at, own_head(at)))
+        for ref, at, value in results:
+            ref[:, at] = value
 
     def cross_heads(first, last):
         usable = mk[...] > 0
-        for j in range(first, last):
-            at = slice(j * HD, (j + 1) * HD)
+
+        def one(j):
+            at = head_at(j)
             scores = jnp.where(usable, scores_of(fx[CQ, :, at], tx[0, :, at]), -jnp.inf)
             weights = jnp.exp(scores - jnp.max(scores, axis=-1, keepdims=True))
             total = jnp.sum(weights, axis=-1, keepdims=True)
             mix = jnp.dot(
                 weights.astype(jnp.bfloat16), tx[1, :, at], preferred_element_type=jnp.float32
             )
-            outc[:, at] = (mix / total).astype(jnp.bfloat16)
+            return at, (mix / total).astype(jnp.bfloat16)
+
+        def step(s, carry):
+            done = [one(first + s * CROSS + i) for i in range(CROSS)]
+            for at, value in done:
+                outc[:, at] = value
+            return carry
+
+        lax.fori_loop(0, (last - first) // CROSS, step, 0)
+        for j in range(last - (last - first) % CROSS, last):
+            at, value = one(j)
+            outc[:, at] = value
 
     def out_at(dst, at):
-        return dst.at[0, :, pl.ds(pl.multiple_of(h * hcols + at.start, HD), at.stop - at.start)]
+        return dst.at[0, :, pl.ds(pl.multiple_of(h * hcols + at.start, HD), at.size)]
 
     def rows_of(src, who, at):
         return src.at[pl.ds(pl.multiple_of(who * rows, rows), rows), at]
@@ -516,7 +537,7 @@
             wait_bytes(src.at[pl.ds(0, rows * (n_head - 1)), at], send)
 
     def send_cross():
-        send_out(outc, co, slice(0, hcols), sent.at[1], out_in.at[1])
+        send_out(outc, co, every, sent.at[1], out_in.at[1])
 
     def wait_text():
         wait_bytes(mk, t_in.at[0])
@@ -547,7 +568,7 @@
         wait_bytes(fx.at[pl.ds(FK, 2)], x_in.at[2])
         lanes = lax.broadcasted_iota(jnp.int32, (prows, HD), 1)
         lse = jnp.zeros((prows, HD), jnp.float32)
-        for j in range(starts[direct], heads):
+        for j in range(direct * cheads, heads):
             at = slice(j * HD, (j + 1) * HD)
             scores = scores_of(fx[FQ, :, at], fx[FK, :, at])
             top = jnp.max(scores, axis=-1, keepdims=True)
@@ -563,10 +584,15 @@
         wait_bytes(fx.at[CQ], x_in.at[0])
         cross_heads(0, heads)
         send_cross()
-        for c in range(direct):
+
+        def direct_chunk(c, carry):
             wait_bytes(kv.at[pl.ds(END, 3), :, :, cols(c)], far_in.at[c])
-            attend_own(c)
+            attend(c, False)
             send_out(outs, so, cols(c), sent.at[6], out_in.at[0])
+            return carry
+
+        if direct:
+            lax.fori_loop(0, direct, direct_chunk, 0)
         wait_bytes(kv.at[END], sent.at[2])
         wait_bytes(dq.at[:, late], sent.at[3])
         wait_bytes(part.at[:, late], sent.at[4])
@@ -619,30 +645,38 @@
         wait_bytes(fx.at[FQ], x_in.at[1])
         wait_bytes(fx.at[pl.ds(FK, 2)], x_in.at[2])
         wait_bytes(kv.at[ACROSS, :, :, late], across_in.at[1])
-        for c in range(direct):
+        def own_chunk(c, carry):
             far = kv.at[FAR, :, :, cols(c)]
             wait_bytes(far, far_in.at[c])
             pass_out(far, FAR, c)
-            attend_own(c)
+            attend(c, False)
             send_out(outs, so, cols(c), sent.at[5], out_in.at[0])
-        wait_bytes(dq.at[:, late], q_in.at[0])
-        wait_bytes(part.at[:, late], part_in.at[0])
-        wait_bytes(stat.at[0], part_in.at[1])
-        for c in range(direct, nch):
+            return carry
+
+        def both_chunk(c, carry):
             wait_bytes(kv.at[FAR, :, :, cols(c)], far_in.at[c])
-            attend_end(c)
+            attend(c, True)
             for k in range(n_head - 1, -1, -1):
                 to = lax.rem(h + k, n_head)
                 remote(
                     rows_of(oute, to, cols(c)), out_at(so, cols(c)),
                     sent.at[4], out_in.at[0], patch=outer, head=to,
                 ).start()
-            attend_own(c)
             send_out(outs, so, cols(c), sent.at[5], out_in.at[0])
+            return carry
+
+        if direct:
+            lax.fori_loop(0, direct, own_chunk, 0)
+        wait_bytes(stat.at[0], part_in.at[1])
+        for j in range(direct * cheads, heads):
+            spread[j] = jnp.broadcast_to(stat[0, :, j : j + 1], (prows, HD))
+        wait_bytes(dq.at[:, late], q_in.at[0])
+        wait_bytes(part.at[:, late], part_in.at[0])
+        lax.fori_loop(direct, nch, both_chunk, 0)
         wait_bytes(kv.at[ACROSS], sent.at[2])
         wait_bytes(kv.at[FAR], sent.at[3])
         wait_bytes(oute.at[:, late], sent.at[4])
-        wait_peers(outs, slice(0, hcols), sent.at[5])
+        wait_peers(outs, every, sent.at[5])
         if direct:
             wait_bytes(kv.at[pl.ds(END, 3), :, :, early], sent.at[6])
 
@@ -650,7 +684,7 @@
     pl.when(jnp.logical_not(is_end))(middle_program)
     if n_head > 1:
         wait_bytes(fx.at[:, pl.ds(0, rows * (n_head - 1)), :], sent.at[0])
-    wait_peers(outc, slice(0, hcols), sent.at[1])
+    wait_peers(outc, every, sent.at[1])
     wait_bytes(co, out_in.at[1])
     wait_bytes(so, out_in.at[0])
 
@@ -660,7 +694,7 @@
     prows = fq.shape[1] * n_head
     hcols = sk.shape[2]
     heads = hcols // HD
-    nch = len(chunk_sizes(heads))
+    nch = heads // chunk_heads(heads)
     direct = min(DIRECT, nch - 1)
     txt = tk.shape[1]
     dma = pltpu.SemaphoreType.DMA
@@ -679,6 +713,7 @@
             patch,
             patch,
             pltpu.VMEM((2, prows, HD), jnp.float32),
+            pltpu.VMEM((heads, prows, HD), jnp.float32),
             patch,
             patch,
             patch,

time: 27.2 us -> 26.9 us (0.989)
  Pallas kernels: 26.4 us -> 26.1 us
    pallas_call x1, Pallas kernels: 25.6 us -> 25.3 us  [quad_attention(): pl.pallas_call(functools.partial(quad_kernel, n_head, direct), out_shape=...]
where the time goes in v3:
time: 26.9 us; the launch traced here: 26.7 us
  Pallas kernels  26.1 us (97%)
  between operations  0.64 us (2%)
    pallas_call x1, Pallas kernels, quad_attention(): pl.pallas_call(functools.partial(quad_kernel, n_head, direct), out_shape=...  25.3 us
    pallas_call x1, Pallas kernels, store(): pl.pallas_call(store_kernel, out_shape=(jax.ShapeDtypeStruct(a.shape, a.d...  0.74 us

profile of v3, /device:TPU:0, one launch (start us, length us, event | category | flops | bytes accessed | tf_op | source)
XLA Modules:
  0.0 26.7 jit_solution(5395815915301650519)
XLA Ops:
  0.6 25.3 %displaced_attention.1 = (bf16[1,32,2560]{2,1,0:T(8,128)(2,1)S(1)}, bf16[1,32,2560]{2,1,0:T(8,128)(2,1)S(1)}) custom-call(bf16[1,32,2560]{2,1,0:T(8,128)(2,1)} %fq.1, bf16[1,32,2560]{2,1,0:T(8,128)(2,1)} %fk.1, bf16[1,32,2560]{2,1,0:T(8,128)(2,1)} %fv.1, bf16[1,64,1280]{2,1,0:T(8,128)(2,1)} %sk.1, bf16[1,64,1280]{2,1,0:T(8,128)(2,1)} %sv.1, ...), custom_call_target="tpu_custom_call" | custom-call | tf_op jit(solution)/shard_map/displaced_attention/pallas_call | solution.py:703
  26.0 0.7 %store_outputs.1 = (bf16[1,32,2560]{2,1,0:T(8,128)(2,1)}, bf16[1,32,2560]{2,1,0:T(8,128)(2,1)}) custom-call(bf16[1,32,2560]{2,1,0:T(8,128)(2,1)S(1)} %get-tuple-element.4.a, bf16[1,32,2560]{2,1,0:T(8,128)(2,1)S(1)} %get-tuple-element.5.b), custom_call_target="tpu_custom_call" | custom-call | tf_op jit(solution)/shard_map/store_outputs/pallas_call | solution.py:748

commit v4 on v3

--- a/solution.py
+++ b/solution.py
@@ -476,14 +476,18 @@
 
     def end_head(at, lse):
         keys, values = (
-            jnp.concatenate([kv[s, i, :, at] for s in (OWN, ACROSS, FAR)]) for i in range(2)
+            jnp.concatenate([kv[s, i, :, at] for s in (END, ACROSS, FAR, OWN)]) for i in range(2)
         )
         scores = scores_of(dq[:, at], keys)
-        top = jnp.maximum(jnp.max(scores, axis=-1, keepdims=True), lse)
-        mix, total = mix_of(jnp.exp(scores - top[:, :1]), values)
-        theirs = jnp.exp(lse - top)
-        mix = mix + part[:, at].astype(jnp.float32) * theirs
-        return (mix / (total + theirs)).astype(jnp.bfloat16)
+        padding = lax.broadcasted_iota(jnp.int32, scores.shape, 1) < prows
+        scores = jnp.where(padding, -jnp.inf, scores)
+        top = jnp.max(scores, axis=-1, keepdims=True)
+        mix, total = mix_of(jnp.exp(scores - top), values)
+        most = jnp.maximum(top, lse)
+        mine = jnp.exp(top - most)
+        theirs = jnp.exp(lse - most)
+        mix = mix * mine + part[:, at].astype(jnp.float32) * theirs
+        return (mix / (total * mine + theirs)).astype(jnp.bfloat16)
 
     def attend(c, both):
         results = []

time: 26.9 us -> 25.9 us (0.963)
  Pallas kernels: 26.1 us -> 25.1 us
    pallas_call x1, Pallas kernels: 25.3 us -> 24.4 us  [quad_attention(): pl.pallas_call(functools.partial(quad_kernel, n_head, direct), out_shape=...]
where the time goes in v4:
time: 25.9 us; the launch traced here: 25.8 us
  Pallas kernels  25.1 us (97%)
  between operations  0.64 us (2%)
    pallas_call x1, Pallas kernels, quad_attention(): pl.pallas_call(functools.partial(quad_kernel, n_head, direct), out_shape=...  24.4 us
    pallas_call x1, Pallas kernels, store(): pl.pallas_call(store_kernel, out_shape=(jax.ShapeDtypeStruct(a.shape, a.d...  0.74 us

profile of v4, /device:TPU:0, one launch (start us, length us, event | category | flops | bytes accessed | tf_op | source)
XLA Modules:
  0.0 25.8 jit_solution(608935111597362043)
XLA Ops:
  0.6 24.4 %displaced_attention.1 = (bf16[1,32,2560]{2,1,0:T(8,128)(2,1)S(1)}, bf16[1,32,2560]{2,1,0:T(8,128)(2,1)S(1)}) custom-call(bf16[1,32,2560]{2,1,0:T(8,128)(2,1)} %fq.1, bf16[1,32,2560]{2,1,0:T(8,128)(2,1)} %fk.1, bf16[1,32,2560]{2,1,0:T(8,128)(2,1)} %fv.1, bf16[1,64,1280]{2,1,0:T(8,128)(2,1)} %sk.1, bf16[1,64,1280]{2,1,0:T(8,128)(2,1)} %sv.1, ...), custom_call_target="tpu_custom_call" | custom-call | tf_op jit(solution)/shard_map/displaced_attention/pallas_call | solution.py:707
  25.0 0.7 %store_outputs.1 = (bf16[1,32,2560]{2,1,0:T(8,128)(2,1)}, bf16[1,32,2560]{2,1,0:T(8,128)(2,1)}) custom-call(bf16[1,32,2560]{2,1,0:T(8,128)(2,1)S(1)} %get-tuple-element.4.a, bf16[1,32,2560]{2,1,0:T(8,128)(2,1)S(1)} %get-tuple-element.5.b), custom_call_target="tpu_custom_call" | custom-call | tf_op jit(solution)/shard_map/store_outputs/pallas_call | solution.py:752

commit v5 on v4

--- a/solution.py
+++ b/solution.py
@@ -374,7 +374,7 @@
     fq, fk, fv, sk, sv, cq, tk, tv, mask,
     so, co,
     fx, kv, tx, mk, dq, part, stat, spread, outs, oute, outc,
-    x_in, t_in, own_in, end_in, far_in, across_in, q_in, part_in, out_in, sent,
+    x_in, t_in, own_in, end_in, far_in, across_in, q_in, part_in, out_in, sent, ready,
 ):
     p = lax.axis_index("patch")
     h = lax.axis_index("head")
@@ -426,26 +426,28 @@
         pltpu.make_async_copy(tv.at[0], tx.at[1], t_in.at[1]).start()
 
     barrier = pltpu.get_barrier_semaphore()
-    for k in range(1, n_head):
-        pl.semaphore_signal(
-            barrier, inc=1, device_id={"head": lax.rem(h + k, n_head)}, device_id_type=MESH
-        )
+
+    def greet(**to):
+        pl.semaphore_signal(barrier, inc=1, device_id=to, device_id_type=MESH)
 
     @pl.when(is_end)
     def _():
-        pl.semaphore_signal(barrier, inc=1, device_id={"patch": inner}, device_id_type=MESH)
+        for k in range(1, n_head):
+            greet(head=lax.rem(h + k, n_head))
 
     @pl.when(jnp.logical_not(is_end))
     def _():
-        pl.semaphore_signal(barrier, inc=1, device_id={"patch": across}, device_id_type=MESH)
-        pl.semaphore_signal(barrier, inc=1, device_id={"patch": outer}, device_id_type=MESH)
+        greet(patch=across)
+        for k in range(1, n_head):
+            pl.when(h + k < n_head)(functools.partial(greet, head=h + k))
+        greet(patch=outer)
         for i, ref in enumerate((sk, sv)):
             pltpu.make_async_copy(ref.at[0], kv.at[OWN, i], own_in.at[0]).start()
 
     for a in range(4):
         own_copy(a).start()
     load_text()
-    pl.semaphore_wait(barrier, n_head - 1 + jnp.where(is_end, 1, 2))
+    pl.semaphore_wait(barrier, 1 + jnp.where(is_end, n_head - 1, h))
 
     def send_x(a):
         for k in range(1, n_head):
@@ -563,12 +565,17 @@
         send_x(CQ)
         for c in range(1, lead):
             send_kv(c)
+
+        def send_rest():
+            for c in range(lead, nch):
+                send_kv(c)
+
+        pl.when(p != 0)(send_rest)
         wait_bytes(fx.at[FQ], x_in.at[1])
         remote(
             fx.at[FQ, :, late], dq.at[:, late], sent.at[3], q_in.at[0], patch=inner
         ).start()
-        for c in range(lead, nch):
-            send_kv(c)
+        pl.when(p == 0)(send_rest)
         wait_bytes(fx.at[pl.ds(FK, 2)], x_in.at[2])
         lanes = lax.broadcasted_iota(jnp.int32, (prows, HD), 1)
         lse = jnp.zeros((prows, HD), jnp.float32)
@@ -626,12 +633,24 @@
         if direct:
             send_own(early, across_in.at[0])
         send_own(late, across_in.at[1])
+        for k in range(1, n_head):
+
+            @pl.when(h - k >= 0)
+            def _():
+                pl.semaphore_signal(
+                    ready, inc=1, device_id={"head": h - k}, device_id_type=MESH
+                )
+
+        @pl.when(h < n_head - 1)
+        def _():
+            pl.semaphore_wait(ready, n_head - 1 - h)
+
         for a in (CQ, FQ, FK, FV):
             send_x(a)
         wait_bytes(kv.at[OWN], own_in.at[0])
+        pass_across(0)
         for c in range(direct):
             pass_out(kv.at[OWN, :, :, cols(c)], END, c)
-        pass_across(0)
         wait_text()
         wait_bytes(fx.at[CQ], x_in.at[0])
         half = heads // 2
@@ -731,6 +750,7 @@
             dma((2,)),
             dma((2,)),
             dma((7,)),
+            pltpu.SemaphoreType.REGULAR,
         ],
         compiler_params=pltpu.CompilerParams(collective_id=0, has_side_effects=True),
         name="displaced_attention",

time: 25.9 us -> 25.1 us (0.969)
  Pallas kernels: 25.1 us -> 24.3 us
    pallas_call x1, Pallas kernels: 24.4 us -> 23.6 us  [quad_attention(): pl.pallas_call(functools.partial(quad_kernel, n_head, direct), out_shape=...]
where the time goes in v5:
time: 25.1 us; the launch traced here: 24.9 us
  Pallas kernels  24.3 us (97%)
  between operations  0.64 us (3%)
    pallas_call x1, Pallas kernels, quad_attention(): pl.pallas_call(functools.partial(quad_kernel, n_head, direct), out_shape=...  23.6 us
    pallas_call x1, Pallas kernels, store(): pl.pallas_call(store_kernel, out_shape=(jax.ShapeDtypeStruct(a.shape, a.d...  0.74 us

profile of v5, /device:TPU:0, one launch (start us, length us, event | category | flops | bytes accessed | tf_op | source)
XLA Modules:
  0.0 24.9 jit_solution(14557733171653593266)
XLA Ops:
  0.6 23.6 %displaced_attention.1 = (bf16[1,32,2560]{2,1,0:T(8,128)(2,1)S(1)}, bf16[1,32,2560]{2,1,0:T(8,128)(2,1)S(1)}) custom-call(bf16[1,32,2560]{2,1,0:T(8,128)(2,1)} %fq.1, bf16[1,32,2560]{2,1,0:T(8,128)(2,1)} %fk.1, bf16[1,32,2560]{2,1,0:T(8,128)(2,1)} %fv.1, bf16[1,64,1280]{2,1,0:T(8,128)(2,1)} %sk.1, bf16[1,64,1280]{2,1,0:T(8,128)(2,1)} %sv.1, ...), custom_call_target="tpu_custom_call" | custom-call | tf_op jit(solution)/shard_map/displaced_attention/pallas_call | solution.py:726
  24.2 0.7 %store_outputs.1 = (bf16[1,32,2560]{2,1,0:T(8,128)(2,1)}, bf16[1,32,2560]{2,1,0:T(8,128)(2,1)}) custom-call(bf16[1,32,2560]{2,1,0:T(8,128)(2,1)S(1)} %get-tuple-element.4.a, bf16[1,32,2560]{2,1,0:T(8,128)(2,1)S(1)} %get-tuple-element.5.b), custom_call_target="tpu_custom_call" | custom-call | tf_op jit(solution)/shard_map/store_outputs/pallas_call | solution.py:772
